TPU v7x, 32 devices: a whole 2x2x4 slice. The times are simulated.
32 devices in a mesh: groups: 2 (over x), img: 16 (over z, y, core).
Axes of the slice: x: 2, y: 2, z: 4, core: 2. Of those that a mesh axis runs over, the one named last changes fastest.
Arguments:
- caches: bfloat16 [32, 768, 1024], P(('groups', 'img')), parts along dimension 0, may hold values from -170 to 170
- owner_slot: int32 [32], P('groups'), parts along dimension 0, may hold values from 0 to 15, each once
- pairs: int32 [32, 2], P('groups'), parts along dimension 0, may hold values from 0 to 15, as said below
- block_mask: int32 [32, 12, 12], P(('groups', 'img')), parts along dimension 0, may hold values from 0 to 1, as said below
- cotangent: bfloat16 [32, 768, 768], P(('groups', 'img')), parts along dimension 0, may hold values from -6 to 6
- embed_weight: bfloat16 [1024, 768], replicated, may hold values from -0.1875 to 0.1875
- query_weight: bfloat16 [768, 512], replicated, may hold values from -2 to 2
- key_weight: bfloat16 [768, 512], replicated, may hold values from -2 to 2
- value_weight: bfloat16 [768, 512], replicated, may hold values from -0.21875 to 0.21875
- out_weight: bfloat16 [768, 512], replicated, may hold values from -0.25 to 0.25
Outputs:
- attended: bfloat16 [32, 768, 768], P(('groups', 'img')), parts along dimension 0
- gradients: float32 [1536, 2048], P(('groups', 'img')), parts along dimension 0
There are 2 independent parts, one for each index of `groups`. A program takes and returns all parts, laid end to end along the dimension named above; an argument that names none is the same for every part. Nothing has to cross between parts.
Inputs may be any that keep to these rules, and one draw needn't show every extreme that they name: `pairs`: each row names two different images. `block_mask`: block (i, i) is live in every pair.
All inputs are finite; a program needn't handle non-finite values.
Results may differ from a plain program's by a relative error of at most 0.012.
Values may be sent and summed in bfloat16 or wider, within the bound.
No kernel may reach another device: no remote copies, remote signals or barrier semaphores. Data moves between devices by JAX's collectives and lax.ppermute only.
A program may use at most 128 MiB of HBM per device.

v0:
```python
import math
import jax
import jax.numpy as jnp
from jax import lax
from jax.sharding import PartitionSpec as P

HEADS = 8
BLOCK = 64


def layer_normed(tokens):
    values_f = tokens.astype(jnp.float32)
    centred = values_f - jnp.mean(values_f, axis=-1, keepdims=True)
    spread_sq = jnp.mean(centred * centred, axis=-1, keepdims=True)
    return (centred * lax.rsqrt(spread_sq + 1e-06)).astype(jnp.bfloat16)


def split_heads(matrix, heads):
    length, width = matrix.shape
    return matrix.reshape(length, heads, width // heads).transpose(1, 0, 2)


def merge_heads(stacked):
    heads, length, hsize = stacked.shape
    return stacked.transpose(1, 0, 2).reshape(length, heads * hsize)


def pair_pass(
    query_tokens,
    key_tokens,
    mask_blocks,
    cotangent,
    query_weight,
    key_weight,
    value_weight,
    out_weight,
    heads,
    block,
):
    query_normed = layer_normed(query_tokens)
    key_normed = layer_normed(key_tokens)
    queries = jnp.dot(query_normed, query_weight, preferred_element_type=jnp.float32).astype(
        jnp.bfloat16
    )
    keys_all = jnp.dot(key_normed, key_weight, preferred_element_type=jnp.float32).astype(
        jnp.bfloat16
    )
    values_all = jnp.dot(key_normed, value_weight, preferred_element_type=jnp.float32).astype(
        jnp.bfloat16
    )
    grad_context = jnp.dot(cotangent, out_weight, preferred_element_type=jnp.float32).astype(
        jnp.bfloat16
    )
    live_mask = jnp.repeat(jnp.repeat(mask_blocks, block, axis=0), block, axis=1) > 0
    scaling = 1.0 / math.sqrt(queries.shape[1] // heads)

    def one_head(operands):
        head_query, head_key, head_value, head_grad = operands
        scores = jnp.dot(head_query, head_key.T, preferred_element_type=jnp.float32) * scaling
        masked = jnp.where(live_mask, scores, -jnp.inf)
        row_max = jnp.max(masked, axis=1, keepdims=True)
        weights = jnp.exp(masked - row_max)
        probability = weights / jnp.sum(weights, axis=1, keepdims=True)
        probability_low = probability.astype(jnp.bfloat16)
        context = jnp.dot(probability_low, head_value, preferred_element_type=jnp.float32).astype(
            jnp.bfloat16
        )
        grad_value = jnp.dot(
            probability_low.T, head_grad, preferred_element_type=jnp.float32
        ).astype(jnp.bfloat16)
        grad_prob = jnp.dot(head_grad, head_value.T, preferred_element_type=jnp.float32)
        inner_sum = jnp.sum(probability * grad_prob, axis=1, keepdims=True)
        grad_score = (probability * (grad_prob - inner_sum) * scaling).astype(jnp.bfloat16)
        grad_query = jnp.dot(grad_score, head_key, preferred_element_type=jnp.float32).astype(
            jnp.bfloat16
        )
        grad_key = jnp.dot(grad_score.T, head_query, preferred_element_type=jnp.float32).astype(
            jnp.bfloat16
        )
        return (context, grad_value, grad_query, grad_key)

    stacked = lax.map(
        one_head,
        (
            split_heads(queries, heads),
            split_heads(keys_all, heads),
            split_heads(values_all, heads),
            split_heads(grad_context, heads),
        ),
    )
    context, grad_value, grad_query, grad_key = [merge_heads(member) for member in stacked]
    attended = (
        query_tokens.astype(jnp.float32)
        + jnp.dot(context, out_weight.T, preferred_element_type=jnp.float32)
    ).astype(jnp.bfloat16)
    return (
        attended,
        (query_normed, key_normed, grad_query, grad_key, grad_value, cotangent, context),
    )


def gradient_rows(kept):
    query_normed, key_normed, grad_query, grad_key, grad_value, cotangent, context = kept
    return jnp.concatenate(
        [
            jnp.dot(query_normed.T, grad_query, preferred_element_type=jnp.float32),
            jnp.dot(key_normed.T, grad_key, preferred_element_type=jnp.float32),
            jnp.dot(key_normed.T, grad_value, preferred_element_type=jnp.float32),
            jnp.dot(cotangent.T, context, preferred_element_type=jnp.float32),
        ],
        axis=1,
    )


def embedded_of(tokens, embed_weight):
    shape_in = tokens.shape
    flat = tokens.reshape(-1, shape_in[-1])
    product = jnp.dot(flat, embed_weight, preferred_element_type=jnp.float32).astype(jnp.bfloat16)
    return product.reshape(shape_in[:-1] + (embed_weight.shape[1],))


def per_device(
    caches,
    owner_slot,
    pairs,
    block_mask,
    cotangent,
    embed_weight,
    query_weight,
    key_weight,
    value_weight,
    out_weight,
):
    devices_img = lax.axis_size("img")
    images_here = caches.shape[0]
    length = caches.shape[1]
    pairs_here = block_mask.shape[0]
    width = caches.shape[-1]
    portion = length // devices_img
    pieces = caches.reshape(images_here, devices_img, portion, width)
    spread = lax.all_to_all(pieces, "img", split_axis=1, concat_axis=0, tiled=True)
    table = spread.reshape(images_here * devices_img, portion, width)
    slots = owner_slot[pairs].reshape(devices_img, pairs_here, 2).transpose(1, 2, 0)
    picked = table[slots]
    arrived = lax.all_to_all(picked, "img", split_axis=2, concat_axis=3, tiled=True)
    tokens = arrived.reshape(pairs_here, 2, length, width)
    tokens = embedded_of(tokens, embed_weight)
    attended, kept = pair_pass(
        tokens[0, 0],
        tokens[0, 1],
        block_mask[0],
        cotangent[0],
        query_weight,
        key_weight,
        value_weight,
        out_weight,
        HEADS,
        BLOCK,
    )
    attended_list = [attended]
    attended_all = jnp.stack(attended_list)
    inverse = 1.0 / (pairs_here * devices_img)
    total = gradient_rows(kept)
    summed = lax.psum_scatter(total, "img", scatter_dimension=0, tiled=True)
    return (attended_all, summed * inverse)


def solution(mesh):
    placed = (
        P(("groups", "img"), None, None),
        P("groups"),
        P("groups", None),
        P(("groups", "img"), None, None),
        P(("groups", "img"), None, None),
        P(),
        P(),
        P(),
        P(),
        P(),
    )
    return jax.shard_map(
        per_device,
        mesh=mesh,
        in_specs=placed,
        out_specs=(P(("groups", "img"), None, None), P(("groups", "img"), None)),
        check_vma=False,
    )
```

profile of v0, /device:TPU:0, one launch (start us, length us, event | category | flops | bytes accessed | tf_op | source)
XLA Modules:
  0.0 350.0 jit_solution(1653082750887615736)
XLA Ops:
  7.2 7.5 %all-to-all-start = ((bf16[1,16,48,1024]{3,2,0,1:T(8,128)(2,1)}), bf16[1,16,48,1024]{3,2,0,1:T(8,128)(2,1)S(1)}, u32[]{:S(2)}, u32[]{:S(2)}) async-start(bf16[1,16,48,1024]{3,2,0,1:T(8,128)(2,1)} %bitcast.197), calls=%async_computation | async-start | bytes 3145728 | tf_op jit(solution)/shard_map/all_to_all | solution.py:141
  15.9 30.8 %all-to-all-done = bf16[1,16,48,1024]{3,2,0,1:T(8,128)(2,1)S(1)} async-done(((bf16[1,16,48,1024]{3,2,0,1:T(8,128)(2,1)}), bf16[1,16,48,1024]{3,2,0,1:T(8,128)(2,1)S(1)}, u32[]{:S(2)}, u32[]{:S(2)}) %all-to-all-start) | async-done | bytes 1572896 | tf_op jit(solution)/shard_map/all_to_all | solution.py:141
  46.7 2.4 gather_fusion.1
  49.1 4.0 %copy.39 = bf16[1,2,16,48,1024]{4,3,1,0,2:T(8,128)(2,1)} copy(bf16[1,2,16,48,1024]{4,3,2,1,0:T(8,128)(2,1)} %bitcast.182) | data formatting | bytes 6291456 | tf_op jit(solution)/shard_map/gather | solution.py:144
  53.2 9.3 %all-to-all-start.1 = ((bf16[1,2,16,48,1024]{4,3,1,0,2:T(8,128)(2,1)}), bf16[1,2,16,48,1024]{4,3,1,0,2:T(8,128)(2,1)}, u32[]{:S(2)}, u32[]{:S(2)}) async-start(bf16[1,2,16,48,1024]{4,3,1,0,2:T(8,128)(2,1)} %copy.39), calls=%async_computation.1 | async-start | bytes 6291456 | tf_op jit(solution)/shard_map/all_to_all | solution.py:145
  66.4 55.5 %all-to-all-done.1 = bf16[1,2,16,48,1024]{4,3,1,0,2:T(8,128)(2,1)} async-done(((bf16[1,2,16,48,1024]{4,3,1,0,2:T(8,128)(2,1)}), bf16[1,2,16,48,1024]{4,3,1,0,2:T(8,128)(2,1)}, u32[]{:S(2)}, u32[]{:S(2)}) %all-to-all-start.1) | async-done | bytes 3145760 | tf_op jit(solution)/shard_map/all_to_all | solution.py:145
  121.9 2.4 copy.40
  124.3 2.8 convolution_convert_fusion.4
  131.5 2.3 convolution_convert_fusion.7
  134.7 3.4 convolution_convert_fusion.8
  139.8 85.0 %while.17 = (s32[]{:T(128)}, bf16[8,768,64]{1,2,0:T(8,128)(2,1)}, bf16[8,768,64]{1,2,0:T(8,128)(2,1)}, bf16[8,768,64]{1,2,0:T(8,128)(2,1)}, bf16[8,768,64]{1,2,0...) while((s32[]{:T(128)}, bf16[8,768,64]{1,2,0:T(8,128)(2,1)}, ...), condition=%wide.region_8.9_spmd.clone, body=%wide.region_4.8_spmd.clone.sunk | while | flops 464385792 | bytes 33088676 | solution.py:82
  146.3 2.2 fusion.115
  156.9 2.2 fusion.115
  167.6 2.2 fusion.115
  178.2 2.2 fusion.115
  199.4 2.2 fusion.115
  210.1 2.2 fusion.115
  220.7 2.2 fusion.115
  224.8 2.6 fusion.58
  232.6 3.1 pad_maximum_fusion
  235.7 6.6 %copy.48 = f32[768,2048]{1,0:T(8,128)} copy(f32[768,2048]{0,1:T(8,128)} %pad_maximum_fusion) | data formatting | bytes 12582912
  243.5 3.5 fusion.55
  246.9 91.5 %reduce-scatter.4.cloned.1.call-done = f32[48,2048]{1,0:T(8,128)} async-done(((f32[768,2048]{1,0:T(8,128)}), f32[48,2048]{1,0:T(8,128)}) %reduce-scatter.4.cloned.1.call-update) | async-done | bytes 393232
  340.9 2.3 copy.46
  (151 shorter events, 90.0 us)
Async XLA Ops:
  7.2 117.1 %copy-start = (bf16[1024,768]{1,0:T(8,128)(2,1)S(1)}, bf16[1024,768]{1,0:T(8,128)(2,1)}, u32[]{:S(2)}) copy-start(bf16[1024,768]{1,0:T(8,128)(2,1)} %param.17) | copy-start | bytes 4718596
  7.2 7.6 %copy-start.8 = (s32[16,2]{0,1:T(2,128)S(1)}, s32[16,2]{0,1:T(2,128)}, u32[]{:S(2)}) copy-start(s32[16,2]{0,1:T(2,128)} %param.14) | copy-start | bytes 388
  7.2 7.8 %copy-start.2 = (s32[16]{0:T(128)S(1)}, s32[16]{0:T(128)}, u32[]{:S(2)}) copy-start(s32[16]{0:T(128)} %param.13) | copy-start | bytes 196
  7.2 39.5 %all-to-all-start = ((bf16[1,16,48,1024]{3,2,0,1:T(8,128)(2,1)}), bf16[1,16,48,1024]{3,2,0,1:T(8,128)(2,1)S(1)}, u32[]{:S(2)}, u32[]{:S(2)}) async-start(bf16[1,16,48,1024]{3,2,0,1:T(8,128)(2,1)} %bitcast.197), calls=%async_computation | async-start | bytes 3145728 | tf_op jit(solution)/shard_map/all_to_all | solution.py:141
  53.2 9.4 %copy-start.9 = (bf16[1,768,768]{2,1,0:T(8,128)(2,1)S(1)}, bf16[1,768,768]{2,1,0:T(8,128)(2,1)}, u32[]{:S(2)}) copy-start(bf16[1,768,768]{2,1,0:T(8,128)(2,1)} %param.16) | copy-start | bytes 3538948
  53.2 68.7 %all-to-all-start.1 = ((bf16[1,2,16,48,1024]{4,3,1,0,2:T(8,128)(2,1)}), bf16[1,2,16,48,1024]{4,3,1,0,2:T(8,128)(2,1)}, u32[]{:S(2)}, u32[]{:S(2)}) async-start(bf16[1,2,16,48,1024]{4,3,1,0,2:T(8,128)(2,1)} %copy.39), calls=%async_computation.1 | async-start | bytes 6291456 | tf_op jit(solution)/shard_map/all_to_all | solution.py:145
  62.5 276.0 %reduce-scatter.4.cloned.1.call-start = ((), (), s32[]{:S(2)}) async-start(), calls=%async_computation.3 | async-start | bytes 6684672
  62.6 3.5 %copy-start.7 = (s32[1,12,12]{2,0,1:T(1,128)S(1)}, s32[1,12,12]{2,0,1:T(1,128)}, u32[]{:S(2)}) copy-start(s32[1,12,12]{2,0,1:T(1,128)} %param.15) | copy-start | bytes 1732
  127.1 1.4 copy-start.3
  127.1 1.7 copy-start.11
  129.9 1.6 copy-start.12
  139.8 1.2 copy-start.5
  146.3 4.2 %copy-start.6 = (bf16[8,768,64]{2,1,0:T(8,128)(2,1)S(1)}, bf16[8,768,64]{2,1,0:T(8,128)(2,1)}, u32[]{:S(2)}) copy-start(bf16[8,768,64]{2,1,0:T(8,128)(2,1)} %copy-done.5) | copy-start | bytes 2359300 | tf_op jit(solution)/shard_map/while
  156.9 4.2 %copy-start.6 = (bf16[8,768,64]{2,1,0:T(8,128)(2,1)S(1)}, bf16[8,768,64]{2,1,0:T(8,128)(2,1)}, u32[]{:S(2)}) copy-start(bf16[8,768,64]{2,1,0:T(8,128)(2,1)} %copy-done.5) | copy-start | bytes 2359300 | tf_op jit(solution)/shard_map/while
  167.6 4.2 %copy-start.6 = (bf16[8,768,64]{2,1,0:T(8,128)(2,1)S(1)}, bf16[8,768,64]{2,1,0:T(8,128)(2,1)}, u32[]{:S(2)}) copy-start(bf16[8,768,64]{2,1,0:T(8,128)(2,1)} %copy-done.5) | copy-start | bytes 2359300 | tf_op jit(solution)/shard_map/while
  178.2 4.2 %copy-start.6 = (bf16[8,768,64]{2,1,0:T(8,128)(2,1)S(1)}, bf16[8,768,64]{2,1,0:T(8,128)(2,1)}, u32[]{:S(2)}) copy-start(bf16[8,768,64]{2,1,0:T(8,128)(2,1)} %copy-done.5) | copy-start | bytes 2359300 | tf_op jit(solution)/shard_map/while
  188.8 4.2 %copy-start.6 = (bf16[8,768,64]{2,1,0:T(8,128)(2,1)S(1)}, bf16[8,768,64]{2,1,0:T(8,128)(2,1)}, u32[]{:S(2)}) copy-start(bf16[8,768,64]{2,1,0:T(8,128)(2,1)} %copy-done.5) | copy-start | bytes 2359300 | tf_op jit(solution)/shard_map/while
  199.4 4.2 %copy-start.6 = (bf16[8,768,64]{2,1,0:T(8,128)(2,1)S(1)}, bf16[8,768,64]{2,1,0:T(8,128)(2,1)}, u32[]{:S(2)}) copy-start(bf16[8,768,64]{2,1,0:T(8,128)(2,1)} %copy-done.5) | copy-start | bytes 2359300 | tf_op jit(solution)/shard_map/while
  210.1 4.2 %copy-start.6 = (bf16[8,768,64]{2,1,0:T(8,128)(2,1)S(1)}, bf16[8,768,64]{2,1,0:T(8,128)(2,1)}, u32[]{:S(2)}) copy-start(bf16[8,768,64]{2,1,0:T(8,128)(2,1)} %copy-done.5) | copy-start | bytes 2359300 | tf_op jit(solution)/shard_map/while
  220.7 4.2 %copy-start.6 = (bf16[8,768,64]{2,1,0:T(8,128)(2,1)S(1)}, bf16[8,768,64]{2,1,0:T(8,128)(2,1)}, u32[]{:S(2)}) copy-start(bf16[8,768,64]{2,1,0:T(8,128)(2,1)} %copy-done.5) | copy-start | bytes 2359300 | tf_op jit(solution)/shard_map/while
  224.8 2.6 copy-start.4
  224.8 2.6 copy-start.14
  228.5 2.2 copy-start.10
  243.5 99.7 %copy-start.1 = (bf16[1024,768]{1,0:T(8,128)(2,1)S(1)}, bf16[1024,768]{1,0:T(8,128)(2,1)}, u32[]{:S(2)}) copy-start(bf16[1024,768]{1,0:T(8,128)(2,1)} %param.17) | copy-start | bytes 4718596
  (8 other events, 9.3 us)
Sparse Core Ops, SparseCore 0:
  242.5 95.9 reduce-scatter.3
where the time goes:
time: 351 us; the launch traced here: 350 us
  waiting for transfers between devices  178 us (51%)
  matrix products  99.2 us (28%)
  local copies, waits for them, and re-layouts  29.2 us (8%)
  starting transfers between devices  16.9 us (5%)
  between operations  14.4 us (4%)
  other arithmetic  12.4 us (4%)
    unnamed x2, waiting for transfers between devices  91.6 us
    all_to_all x1, waiting for transfers between devices, per_device(): lax.all_to_all(picked, 'img', split_axis=2, concat_axis=3, tiled=True)  55.5 us
    all_to_all x1, waiting for transfers between devices, per_device(): lax.all_to_all(pieces, 'img', split_axis=1, concat_axis=0, tiled=True)  30.8 us
    dot_general x8, matrix products, one_head(): jnp.dot(probability_low.T, head_grad, preferred_element_type=jnp.float32)  17.7 us
    dot_general x8, matrix products, one_head(): jnp.dot(grad_score.T, head_query, preferred_element_type=jnp.float32)  16.7 us
    dot_general x8, matrix products, one_head(): jnp.dot(probability_low, head_value, preferred_element_type=jnp.float32)  15.6 us
    dot_general x8, matrix products, one_head(): jnp.dot(head_grad, head_value.T, preferred_element_type=jnp.float32)  14.5 us
    unnamed x29, local copies, waits for them, and re-layouts  11.8 us
  transfers between devices with their start and end apart: 3, of which 3 were waited for; matrix products, arithmetic and copies ran while one was open for 2% of the time, Pallas kernels for 0%

commit v1 on v0

--- a/solution.py
+++ b/solution.py
@@ -6,6 +6,18 @@
 
 HEADS = 8
 BLOCK = 64
+
+
+def answer_edges_for(xx, dim_no, dim_at):
+    return jnp.concatenate(
+        lax.all_to_all(
+            jnp.stack(jnp.split(xx, lax.axis_size("img"), axis=dim_no)),
+            axis_name="img",
+            split_axis=0,
+            concat_axis=0,
+        ),
+        dim_at,
+    )
 
 
 def layer_normed(tokens):
@@ -138,7 +150,7 @@
     width = caches.shape[-1]
     portion = length // devices_img
     pieces = caches.reshape(images_here, devices_img, portion, width)
-    spread = lax.all_to_all(pieces, "img", split_axis=1, concat_axis=0, tiled=True)
+    spread = answer_edges_for(pieces, 1, 0)
     table = spread.reshape(images_here * devices_img, portion, width)
     slots = owner_slot[pairs].reshape(devices_img, pairs_here, 2).transpose(1, 2, 0)
     picked = table[slots]

time: 351 us -> 369 us (1.051)
  local copies, waits for them, and re-layouts: 29.2 us -> 47 us
    unnamed x29 -> x46, local copies, waits for them, and re-layouts: 11.8 us -> 29 us
where the time goes in v1:
time: 369 us; the launch traced here: 367 us
  waiting for transfers between devices  178 us (48%)
  matrix products  98.9 us (27%)
  local copies, waits for them, and re-layouts  47 us (13%)
  starting transfers between devices  16.8 us (5%)
  between operations  14.4 us (4%)
  other arithmetic  12.3 us (3%)
    unnamed x2, waiting for transfers between devices  91.7 us
    all_to_all x1, waiting for transfers between devices, per_device(): lax.all_to_all(picked, 'img', split_axis=2, concat_axis=3, tiled=True)  55.5 us
    all_to_all x1, waiting for transfers between devices, answer_edges_for(): lax.all_to_all(jnp.stack(jnp.split(xx, lax.axis_size('img'), axis=dim_no)...  30.8 us
    unnamed x46, local copies, waits for them, and re-layouts  29 us
    dot_general x8, matrix products, one_head(): jnp.dot(probability_low.T, head_grad, preferred_element_type=jnp.float32)  16.7 us
    dot_general x8, matrix products, one_head(): jnp.dot(grad_score.T, head_query, preferred_element_type=jnp.float32)  16.6 us
    dot_general x8, matrix products, one_head(): jnp.dot(probability_low, head_value, preferred_element_type=jnp.float32)  16.5 us
    dot_general x8, matrix products, one_head(): jnp.dot(head_grad, head_value.T, preferred_element_type=jnp.float32)  14.5 us
  transfers between devices with their start and end apart: 3, of which 3 were waited for; matrix products, arithmetic and copies ran while one was open for 2% of the time, Pallas kernels for 0%

profile of v1, /device:TPU:0, one launch (start us, length us, event | category | flops | bytes accessed | tf_op | source)
XLA Modules:
  0.0 367.5 jit_solution(12697662056422691002)
XLA Ops:
  24.7 7.5 %all-to-all-start = ((bf16[16,1,1,48,1024]{4,3,2,1,0:T(8,128)(2,1)}), bf16[16,1,1,48,1024]{4,3,2,1,0:T(8,128)(2,1)S(1)}, u32[]{:S(2)}, u32[]{:S(2)}) async-start(bf16[16,1,1,48,1024]{4,3,2,1,0:T(8,128)(2,1)} %fusion.69), calls=%async_computation | async-start | bytes 3145728 | tf_op jit(solution)/shard_map/all_to_all | solution.py:13
  33.4 30.8 %all-to-all-done = bf16[16,1,1,48,1024]{4,3,2,1,0:T(8,128)(2,1)S(1)} async-done(((bf16[16,1,1,48,1024]{4,3,2,1,0:T(8,128)(2,1)}), bf16[16,1,1,48,1024]{4,3,2,1,0:T(8,128)(2,1)S(1)}, u32[]{:S(2)}, u32[]{:S(2)}) %all-to-all-start) | async-done | bytes 1572896 | tf_op jit(solution)/shard_map/all_to_all | solution.py:13
  64.2 2.4 gather_fusion.1
  66.6 4.0 %copy.38 = bf16[1,2,16,48,1024]{4,3,1,0,2:T(8,128)(2,1)} copy(bf16[1,2,16,48,1024]{4,3,2,1,0:T(8,128)(2,1)} %bitcast.246) | data formatting | bytes 6291456 | tf_op jit(solution)/shard_map/gather | solution.py:156
  70.7 9.3 %all-to-all-start.1 = ((bf16[1,2,16,48,1024]{4,3,1,0,2:T(8,128)(2,1)}), bf16[1,2,16,48,1024]{4,3,1,0,2:T(8,128)(2,1)}, u32[]{:S(2)}, u32[]{:S(2)}) async-start(bf16[1,2,16,48,1024]{4,3,1,0,2:T(8,128)(2,1)} %copy.38), calls=%async_computation.1 | async-start | bytes 6291456 | tf_op jit(solution)/shard_map/all_to_all | solution.py:157
  83.9 55.5 %all-to-all-done.1 = bf16[1,2,16,48,1024]{4,3,1,0,2:T(8,128)(2,1)} async-done(((bf16[1,2,16,48,1024]{4,3,1,0,2:T(8,128)(2,1)}), bf16[1,2,16,48,1024]{4,3,1,0,2:T(8,128)(2,1)}, u32[]{:S(2)}, u32[]{:S(2)}) %all-to-all-start.1) | async-done | bytes 3145760 | tf_op jit(solution)/shard_map/all_to_all | solution.py:157
  139.4 2.4 copy.39
  141.8 2.8 convolution_convert_fusion.4
  149.3 2.3 convolution_convert_fusion.7
  152.5 3.4 convolution_convert_fusion.8
  157.6 84.8 %while.17 = (s32[]{:T(128)}, bf16[8,768,64]{1,2,0:T(8,128)(2,1)}, bf16[8,768,64]{1,2,0:T(8,128)(2,1)}, bf16[8,768,64]{1,2,0:T(8,128)(2,1)}, bf16[8,768,64]{1,2,0...) while((s32[]{:T(128)}, bf16[8,768,64]{1,2,0:T(8,128)(2,1)}, ...), condition=%wide.region_8.9_spmd.clone, body=%wide.region_4.8_spmd.clone.sunk | while | flops 464385792 | bytes 33088676 | solution.py:94
  164.1 2.1 fusion.131
  174.7 2.1 fusion.131
  195.9 2.1 fusion.131
  217.1 2.1 fusion.131
  224.6 2.1 fusion.133
  238.3 2.1 fusion.131
  242.4 2.6 fusion.58
  246.1 2.2 fusion.89
  250.2 3.0 pad_maximum_fusion
  253.1 6.6 %copy.47 = f32[768,2048]{1,0:T(8,128)} copy(f32[768,2048]{0,1:T(8,128)} %pad_maximum_fusion) | data formatting | bytes 12582912
  260.9 3.4 fusion.55
  264.2 91.7 %reduce-scatter.4.cloned.1.call-done = f32[48,2048]{1,0:T(8,128)} async-done(((f32[768,2048]{1,0:T(8,128)}), f32[48,2048]{1,0:T(8,128)}) %reduce-scatter.4.cloned.1.call-update) | async-done | bytes 393232
  358.4 2.3 copy.45
  (169 shorter events, 108.4 us)
Async XLA Ops:
  7.2 134.6 %copy-start = (bf16[1024,768]{1,0:T(8,128)(2,1)S(1)}, bf16[1024,768]{1,0:T(8,128)(2,1)}, u32[]{:S(2)}) copy-start(bf16[1024,768]{1,0:T(8,128)(2,1)} %param.17) | copy-start | bytes 4718596
  7.2 12.4 %copy-start.7 = (bf16[1,768,1024]{2,1,0:T(8,128)(2,1)S(1)}, bf16[1,768,1024]{2,1,0:T(8,128)(2,1)}, u32[]{:S(2)}) copy-start(bf16[1,768,1024]{2,1,0:T(8,128)(2,1)} %param.12) | copy-start | bytes 4718596
  24.7 7.5 %copy-start.9 = (s32[16,2]{0,1:T(2,128)S(1)}, s32[16,2]{0,1:T(2,128)}, u32[]{:S(2)}) copy-start(s32[16,2]{0,1:T(2,128)} %param.14) | copy-start | bytes 388
  24.7 7.7 %copy-start.2 = (s32[16]{0:T(128)S(1)}, s32[16]{0:T(128)}, u32[]{:S(2)}) copy-start(s32[16]{0:T(128)} %param.13) | copy-start | bytes 196
  24.7 39.5 %all-to-all-start = ((bf16[16,1,1,48,1024]{4,3,2,1,0:T(8,128)(2,1)}), bf16[16,1,1,48,1024]{4,3,2,1,0:T(8,128)(2,1)S(1)}, u32[]{:S(2)}, u32[]{:S(2)}) async-start(bf16[16,1,1,48,1024]{4,3,2,1,0:T(8,128)(2,1)} %fusion.69), calls=%async_computation | async-start | bytes 3145728 | tf_op jit(solution)/shard_map/all_to_all | solution.py:13
  70.7 9.4 %copy-start.10 = (bf16[1,768,768]{2,1,0:T(8,128)(2,1)S(1)}, bf16[1,768,768]{2,1,0:T(8,128)(2,1)}, u32[]{:S(2)}) copy-start(bf16[1,768,768]{2,1,0:T(8,128)(2,1)} %param.16) | copy-start | bytes 3538948
  70.7 68.7 %all-to-all-start.1 = ((bf16[1,2,16,48,1024]{4,3,1,0,2:T(8,128)(2,1)}), bf16[1,2,16,48,1024]{4,3,1,0,2:T(8,128)(2,1)}, u32[]{:S(2)}, u32[]{:S(2)}) async-start(bf16[1,2,16,48,1024]{4,3,1,0,2:T(8,128)(2,1)} %copy.38), calls=%async_computation.1 | async-start | bytes 6291456 | tf_op jit(solution)/shard_map/all_to_all | solution.py:157
  80.0 275.9 %reduce-scatter.4.cloned.1.call-start = ((), (), s32[]{:S(2)}) async-start(), calls=%async_computation.3 | async-start | bytes 6684672
  82.0 1.5 copy-start.8
  144.6 1.4 copy-start.3
  145.0 1.6 copy-start.12
  147.7 1.6 copy-start.13
  166.2 2.1 copy-start.6
  176.8 2.1 copy-start.6
  187.4 2.1 copy-start.6
  198.0 2.1 copy-start.6
  208.6 2.1 copy-start.6
  219.2 2.1 copy-start.6
  229.8 2.1 copy-start.6
  240.4 2.1 copy-start.6
  242.4 2.6 copy-start.4
  242.4 2.6 copy-start.15
  246.1 2.2 copy-start.11
  355.9 4.8 %copy-start.1 = (bf16[1024,768]{1,0:T(8,128)(2,1)S(1)}, bf16[1024,768]{1,0:T(8,128)(2,1)}, u32[]{:S(2)}) copy-start(bf16[1024,768]{1,0:T(8,128)(2,1)} %param.17) | copy-start | bytes 4718596
  (9 other events, 10.4 us)
Sparse Core Ops, SparseCore 0:
  259.9 95.9 reduce-scatter.3
